TPU v7x, 512 devices: a whole 4x4x16 slice. The times are simulated.
512 devices in a mesh: tm: 128 (over z, y, core), mod: 4 (over x).
Axes of the slice: x: 4, y: 4, z: 16, core: 2. Of those that a mesh axis runs over, the one named last changes fastest.
Arguments:
- filterbank: bfloat16 [16384, 128], P('tm'), may hold values from -6 to 6
- conv_weight: bfloat16 [384, 1280], replicated, may hold values from -0.3125 to 0.3125
- mlp_gain: float32 [1280], replicated, may hold values from 0.25 to 1.75
- up_weight: bfloat16 [1280, 5120], P('tm', 'mod'), may hold values from -0.15625 to 0.15625
- down_weight: bfloat16 [5120, 1280], P('mod', 'tm'), may hold values from -0.078125 to 0.078125
- post_gain: float32 [1280], replicated, may hold values from 0.25 to 1.75
- audio_weight: bfloat16 [1280, 1792], P(None, 'mod'), may hold values from -0.15625 to 0.15625
- patches: bfloat16 [32768, 1280], P('tm'), may hold values from -6 to 6
- vision_gain: float32 [1280], replicated, may hold values from 0.25 to 1.75
- vision_weight: bfloat16 [5120, 1792], P('tm', 'mod'), may hold values from -0.078125 to 0.078125
- retention: int32 [128, 64], P('tm'), may hold values from 0 to 63, each once within a row
- kept_count: int32 [128], P('tm'), may hold values from 1 to 64, 4096 in all
Outputs:
- sequence: bfloat16 [128, 96, 1792], P('tm', None, 'mod')
Inputs may be any that keep to these rules, and one draw needn't show every extreme that they name: `retention`: each row lists every merged token of its frame once. `kept_count`: the counts sum to 4096.
All inputs are finite; a program needn't handle non-finite values. No bound on the sum of `kept_count` on one device may be relied on, other than what follows from the above.
Results may differ from a plain program's by a relative error of at most 0.01.
Values may be sent and summed in bfloat16 or wider, within the bound.
No kernel may reach another device: no remote copies, remote signals or barrier semaphores. Data moves between devices by JAX's collectives and lax.ppermute only.
A program may use at most 64 MiB of HBM per device.

v0:
```python
import jax
import jax.numpy as jnp
from jax import lax
from jax.sharding import PartitionSpec as P

MRG_FRAME = 64
AUD_TOK = 64
SEQ_DEV = 96


def carried_in(value, axis, join, neutral):
    count, mine = (lax.axis_size(axis), lax.axis_index(axis))
    pieces = lax.all_gather(value, axis)
    running = jnp.full_like(value, 0) + jnp.asarray(neutral, value.dtype)

    def hop(position, running):
        longer = join(running, pieces[position])
        return jnp.where(position < mine, longer, running)

    return lax.fori_loop(0, count - 1, hop, running)


def padded(shard, sides, width):
    for axis, dim in sides:
        peers, length = (lax.axis_size(axis), shard.shape[dim])
        up = [(i, (i + 1) % peers) for i in range(peers - 1)]
        down = [(j, i) for i, j in up]
        last = lax.slice_in_dim(shard, length - width, length, axis=dim)
        first = lax.slice_in_dim(shard, 0, width, axis=dim)
        before = lax.ppermute(last, axis, up)
        after = lax.ppermute(first, axis, down)
        shard = jnp.concatenate([before, shard, after], axis=dim)
    return shard


def layer_norm(values, scale_gain):
    average = jnp.mean(values, axis=-1, keepdims=True)
    centred = values - average
    variance = jnp.mean(centred * centred, axis=-1, keepdims=True)
    return centred * lax.rsqrt(variance + 1e-05) * scale_gain


def rms_norm(values, scale_gain):
    square_mean = jnp.mean(values * values, axis=-1, keepdims=True)
    return values * lax.rsqrt(square_mean + 1e-06) * scale_gain


def pool_pairs(values):
    return values.reshape(-1, 2, values.shape[-1]).mean(axis=1)


def add_counts(earlier, later):
    return earlier + later


def on_device(
    filterbank,
    conv_weight,
    mlp_gain,
    up_weight,
    down_weight,
    post_gain,
    audio_weight,
    patches,
    vision_gain,
    vision_weight,
    retention,
    kept_count,
):
    placed = kept_count + AUD_TOK
    starts = carried_in(placed, "tm", add_counts, jnp.zeros((1,), jnp.int32))
    framed = padded(filterbank, (("tm", 0),), 1)
    unfolded = jnp.concatenate([framed[:-2], framed[1:-1], framed[2:]], axis=1)
    stem = jax.nn.gelu(
        jnp.dot(unfolded, conv_weight, preferred_element_type=jnp.float32), approximate=False
    ).astype(jnp.bfloat16)
    residual = stem.astype(jnp.float32)
    hidden = layer_norm(residual, mlp_gain).astype(jnp.bfloat16)
    up_share = lax.all_gather(up_weight, "tm", axis=0, tiled=True)
    pre_act = jnp.dot(hidden, up_share, preferred_element_type=jnp.float32)
    activated = jax.nn.gelu(pre_act, approximate=False).astype(jnp.bfloat16)
    down_share = lax.all_gather(down_weight, "tm", axis=1, tiled=True)
    partial_value = jnp.dot(activated, down_share, preferred_element_type=jnp.float32)
    summed = lax.psum(partial_value.astype(jnp.bfloat16), "mod").astype(jnp.float32)
    pooled = pool_pairs(residual + summed)
    normed = layer_norm(pooled, post_gain).astype(jnp.bfloat16)
    audio_tokens = jnp.dot(normed, audio_weight, preferred_element_type=jnp.float32).astype(
        jnp.bfloat16
    )
    patch_normed = rms_norm(patches.astype(jnp.float32), vision_gain).astype(jnp.bfloat16)
    merged = patch_normed.reshape(-1, 4 * patch_normed.shape[1])
    vision_share = lax.all_gather(vision_weight, "tm", axis=0, tiled=True)
    visual_tokens = jnp.dot(merged, vision_share, preferred_element_type=jnp.float32).astype(
        jnp.bfloat16
    )
    peer_count = lax.axis_size("tm")
    per_peer = (AUD_TOK + MRG_FRAME + peer_count - 1) // peer_count
    kept_here = kept_count[0]
    first_slot = starts[0]
    all_tokens = jnp.concatenate([visual_tokens, audio_tokens], axis=0)
    peer_ids = jnp.arange(peer_count, dtype=jnp.int32)[:, None]
    round_ids = jnp.arange(per_peer, dtype=jnp.int32)[None, :]
    local_index = round_ids * peer_count + (peer_ids - first_slot) % peer_count
    valid_rows = local_index < kept_here + AUD_TOK
    kept_index = jnp.take(retention[0], jnp.minimum(local_index, MRG_FRAME - 1), axis=0)
    source_index = jnp.where(
        local_index < kept_here, kept_index, MRG_FRAME + local_index - kept_here
    )
    source_index = jnp.where(valid_rows, source_index, 0).astype(jnp.int32)
    send_rows = jnp.take(all_tokens, source_index.reshape(-1), axis=0).reshape(
        peer_count, per_peer, all_tokens.shape[1]
    )
    send_slots = jnp.where(valid_rows, (first_slot + local_index) // peer_count, SEQ_DEV).astype(
        jnp.int32
    )
    recv_rows, recv_slots = (
        lax.all_to_all(send_rows, "tm", split_axis=0, concat_axis=0, tiled=True),
        lax.all_to_all(send_slots, "tm", split_axis=0, concat_axis=0, tiled=True),
    )
    sequence = jnp.zeros((SEQ_DEV, all_tokens.shape[1]), jnp.bfloat16)
    sequence = sequence.at[recv_slots.reshape(-1)].set(
        recv_rows.reshape(-1, all_tokens.shape[1]), mode="drop"
    )
    return sequence[None]


def solution(mesh):
    return jax.shard_map(
        on_device,
        mesh=mesh,
        in_specs=(
            P("tm", None),
            P(),
            P(),
            P("tm", "mod"),
            P("mod", "tm"),
            P(),
            P(None, "mod"),
            P("tm", None),
            P(),
            P("tm", "mod"),
            P("tm", None),
            P("tm"),
        ),
        out_specs=P("tm", None, "mod"),
        check_vma=False,
    )
```

profile of v0, /device:TPU:1, one launch (start us, length us, event | category | flops | bytes accessed | tf_op | source)
XLA Modules:
  0.0 566.4 jit_solution(12969941539579024190)
XLA Ops:
  6.5 0.7 all-gather.9.cloned.1.call-update
  7.3 0.7 all-gather.11.cloned.1.call-update
  8.1 0.7 fusion.127
  8.8 4.6 collective-permute-start
  13.3 5.5 collective-permute-start.1
  18.8 0.8 collective-permute-done.1
  19.6 3.0 convert_reduce_fusion
  22.8 136.3 %all-gather.9.cloned.1.call-done = bf16[128,10,1280]{2,1,0:T(8,128)(2,1)} async-done(((bf16[1,10,1280]{2,1,0:T(8,128)(2,1)}), bf16[128,10,1280]{2,1,0:T(8,128)(2,1)}) %all-gather.9.cloned.1.call-update) | async-done | bytes 3276816 | tf_op jit(solution)/shard_map/all_gather | solution.py:79
  159.1 7.0 %reshape.396 = bf16[1280,1280]{1,0:T(8,128)(2,1)} reshape(bf16[128,10,1280]{2,1,0:T(8,128)(2,1)} %all-gather.9.cloned.1.call-done) | data formatting | bytes 6553600
  166.2 134.5 %all-gather.11.cloned.1.call-done = bf16[128,10,1280]{2,1,0:T(8,128)(2,1)} async-done(((bf16[1,10,1280]{2,1,0:T(8,128)(2,1)}), bf16[128,10,1280]{2,1,0:T(8,128)(2,1)}) %all-gather.11.cloned.1.call-update) | async-done | bytes 3276816 | tf_op jit(solution)/shard_map/all_gather | solution.py:82
  300.7 7.0 %reshape.398 = bf16[1280,1280]{1,0:T(8,128)(2,1)} reshape(bf16[128,10,1280]{2,1,0:T(8,128)(2,1)} %all-gather.11.cloned.1.call-done) | data formatting | bytes 6553600
  307.7 6.5 %convolution_convert_fusion = bf16[128,1280]{1,0:T(8,128)(2,1)} fusion(bf16[1280,1280]{1,0:T(8,128)(2,1)} %reshape.398, bf16[1280,1280]{1,0:T(8,128)(2,1)} %reshape.396, bf16[128,1280]{1,0:T(8,128)(2,1)S(1)} %get-tuple-element.96, f32[1280]{0:T(1024)S(1)} %copy-done.5, f32[128]{0:T(128)S(1)} %add_rsqrt_fusion.2, f32[128]{0:T(128)S(1)} %broadcast_multiply_fusion.1), kind=kOutput, calls=%fused_computation.4 | convolution fusion | flops 850493440 | bytes 7215104 | tf_op jit(solution)/shard_map/dot_general | solution.py:83
  315.5 1.3 dynamic-slice
  316.8 0.7 add_dynamic-update-slice_fusion
  317.5 20.8 %all-reduce = s32[128]{0:T(128)S(1)} all-reduce(s32[128]{0:T(128)S(1)} %add_dynamic-update-slice_fusion), channel_id=2, replica_groups=mesh['tm'=128,'mod'=4] {'tm'}, use_global_device_ids=true, to_apply=%add | all-reduce | flops 128 | bytes 1024
  338.3 157.1 %while.13 = (s32[]{:T(128)}, s32[1]{0:T(128)}, s32[]{:T(128)}, s32[128,1]{0,1:T(1,128)S(1)}, s32[]{:T(128)}) while((s32[]{:T(128)}, s32[1]{0:T(128)}, s32[]{:T(128)}, s32[128,1]{0,1:T(1,128)S(1)}, s32[]{:T(128)}) %tuple.41), condition=%wide.region_1.2_spmd, body=%wide.region_0.1_spmd.sunk | while | flops 5 | bytes 107 | solution.py:20
  339.6 0.6 constant_dynamic-slice_fusion.2
  345.8 0.6 constant_dynamic-slice_fusion.2
  348.2 0.6 constant_dynamic-slice_fusion.2
  354.4 0.6 constant_dynamic-slice_fusion.2
  363.1 0.6 constant_dynamic-slice_fusion.2
  369.3 0.6 constant_dynamic-slice_fusion.2
  371.7 0.6 constant_dynamic-slice_fusion.2
  377.9 0.6 constant_dynamic-slice_fusion.2
  386.6 0.6 constant_dynamic-slice_fusion.2
  392.8 0.6 constant_dynamic-slice_fusion.2
  395.3 0.6 constant_dynamic-slice_fusion.2
  401.4 0.6 constant_dynamic-slice_fusion.2
  410.1 0.6 constant_dynamic-slice_fusion.2
  416.3 0.6 constant_dynamic-slice_fusion.2
  418.8 0.6 constant_dynamic-slice_fusion.2
  424.9 0.6 constant_dynamic-slice_fusion.2
  429.9 0.6 constant_dynamic-slice_fusion.2
  438.6 0.6 constant_dynamic-slice_fusion.2
  495.5 1.2 compare_select_fusion.3
  496.7 15.0 %all-to-all-start = ((s32[128,1,1]{2,1,0:T(1,128)}), s32[128,1,1]{2,1,0:T(1,128)S(1)}, u32[]{:S(2)}, u32[]{:S(2)}) async-start(s32[128,1,1]{2,1,0:T(1,128)} %compare_select_fusion.3), calls=%async_computation | async-start | bytes 131072 | tf_op jit(solution)/shard_map/all_to_all | solution.py:118
  512.5 2.5 fusion.89
  515.0 1.2 gather_fusion
  516.3 1.0 convert_add_fusion
  517.8 0.8 reduce_sum.57
  519.4 3.5 convolution_convert_fusion.2
  523.0 0.8 gather_fusion.1
  524.5 0.7 reduce.3
  525.2 0.8 reshape.405
  526.5 15.6 %all-to-all-start.1 = ((bf16[128,2,224]{2,1,0:T(2,128)(2,1)}), bf16[128,2,224]{2,1,0:T(2,128)(2,1)S(1)}, u32[]{:S(2)}, u32[]{:S(2)}) async-start(bf16[128,2,224]{2,1,0:T(2,128)(2,1)} %reshape.405), calls=%async_computation.1 | async-start | bytes 262144 | tf_op jit(solution)/shard_map/all_to_all | solution.py:117
  542.1 2.4 reduce
  544.5 13.6 %all-to-all-done.1 = bf16[128,2,224]{2,1,0:T(2,128)(2,1)S(1)} async-done(((bf16[128,2,224]{2,1,0:T(2,128)(2,1)}), bf16[128,2,224]{2,1,0:T(2,128)(2,1)S(1)}, u32[]{:S(2)}, u32[]{:S(2)}) %all-to-all-start.1) | async-done | bytes 114720 | tf_op jit(solution)/shard_map/all_to_all | solution.py:117
  558.3 1.6 scatter_custom_fusion
  (154 shorter events, 69.2 us)
Async XLA Ops:
  6.5 512.4 %copy-start = (bf16[1280,448]{0,1:T(8,128)(2,1)S(1)}, bf16[1280,448]{0,1:T(8,128)(2,1)}, u32[]{:S(2)}) copy-start(bf16[1280,448]{0,1:T(8,128)(2,1)} %param.20) | copy-start | bytes 3440644
  6.5 152.6 %all-gather.9.cloned.1.call-start = ((), (), s32[]{:S(2)}) async-start(), calls=%async_computation.4 | async-start | bytes 5283840 | tf_op jit(solution)/shard_map/all_gather | solution.py:79
  7.3 293.4 %all-gather.11.cloned.1.call-start = ((), (), s32[]{:S(2)}) async-start(), calls=%async_computation.5 | async-start | bytes 5283840 | tf_op jit(solution)/shard_map/all_gather | solution.py:82
  8.0 508.3 %all-reduce.3.cloned.1.call-start = ((), (), s32[]{:S(2)}) async-start(), calls=%async_computation.3 | async-start | bytes 655360 | tf_op jit(solution)/shard_map/psum | solution.py:84
  8.8 10.0 %collective-permute-start = (bf16[1,128]{1,0:T(2,128)(2,1)S(1)}, bf16[1,128]{1,0:T(2,128)(2,1)S(1)}, u32[]{:S(2)}, u32[]{:S(2)}) collective-permute-start(bf16[1,128]{1,0:T(2,128)(2,1)S(1)} %get-tuple-element.93), channel_id=1, source_target_pairs={{0,4},{4,8},{8,12},{12,16},{16,20},{20,24},{24,28},{28,32},{32,36}... | collective-permute-start | bytes 776 | tf_op jit(solution)/shard_map/ppermute | solution.py:30
  13.3 6.3 %collective-permute-start.1 = (bf16[1,128]{1,0:T(2,128)(2,1)S(1)}, bf16[1,128]{1,0:T(2,128)(2,1)S(1)}, u32[]{:S(2)}, u32[]{:S(2)}) collective-permute-start(bf16[1,128]{1,0:T(2,128)(2,1)S(1)} %get-tuple-element.94), channel_id=1, source_target_pairs={{4,0},{8,4},{12,8},{16,12},{20,16},{24,20},{28,24},{32,28},{36,32}... | collective-permute-start | bytes 776 | tf_op jit(solution)/shard_map/ppermute | solution.py:31
  166.2 141.6 %copy-start.5 = (f32[1280]{0:T(1024)S(1)}, f32[1280]{0:T(1024)}, u32[]{:S(2)}) copy-start(f32[1280]{0:T(1024)} %param.16) | copy-start | bytes 15364
  307.7 203.9 %copy-start.2 = (bf16[256,1280]{1,0:T(8,128)(2,1)S(1)}, bf16[256,1280]{1,0:T(8,128)(2,1)}, u32[]{:S(2)}) copy-start(bf16[256,1280]{1,0:T(8,128)(2,1)} %param.21) | copy-start | bytes 1966084
  307.7 204.2 %copy-start.3 = (f32[1280]{0:T(1024)S(1)}, f32[1280]{0:T(1024)}, u32[]{:S(2)}) copy-start(f32[1280]{0:T(1024)} %param.22) | copy-start | bytes 15364
  314.3 200.8 %copy-start.1 = (s32[1,64]{1,0:T(1,128)S(1)}, s32[1,64]{1,0:T(1,128)}, u32[]{:S(2)}) copy-start(s32[1,64]{1,0:T(1,128)} %param.24) | copy-start | bytes 772
  314.3 205.1 %all-gather.7.cloned.1.call-start = ((), (), s32[]{:S(2)}) async-start(), calls=%async_computation.2 | async-start | bytes 5283840 | tf_op jit(solution)/shard_map/all_gather | solution.py:92
  496.7 29.9 %all-to-all-start = ((s32[128,1,1]{2,1,0:T(1,128)}), s32[128,1,1]{2,1,0:T(1,128)S(1)}, u32[]{:S(2)}, u32[]{:S(2)}) async-start(s32[128,1,1]{2,1,0:T(1,128)} %compare_select_fusion.3), calls=%async_computation | async-start | bytes 131072 | tf_op jit(solution)/shard_map/all_to_all | solution.py:118
  512.1 6.8 %copy-start.4 = (f32[1280]{0:T(1024)S(1)}, f32[1280]{0:T(1024)}, u32[]{:S(2)}) copy-start(f32[1280]{0:T(1024)} %param.19) | copy-start | bytes 15364
  526.5 31.6 %all-to-all-start.1 = ((bf16[128,2,224]{2,1,0:T(2,128)(2,1)}), bf16[128,2,224]{2,1,0:T(2,128)(2,1)S(1)}, u32[]{:S(2)}, u32[]{:S(2)}) async-start(bf16[128,2,224]{2,1,0:T(2,128)(2,1)} %reshape.405), calls=%async_computation.1 | async-start | bytes 262144 | tf_op jit(solution)/shard_map/all_to_all | solution.py:117
Sparse Core Ops, SparseCore 0:
  10.5 148.6 all-gather.8
  162.3 138.3 all-gather.10
  314.4 50.3 all-reduce.2
  367.8 146.2 all-gather.6
where the time goes:
time: 574 us; the launch traced here: 566 us
  waiting for transfers between devices  288 us (50%)
  local copies, waits for them, and re-layouts  97.5 us (17%)
  loops' own time  81.7 us (14%)
  starting transfers between devices  40.7 us (7%)
  blocking collectives  20.8 us (4%)
  between operations  14 us (2%)
  matrix products  13.5 us (2%)
  other arithmetic  10.4 us (2%)
    all_gather x1, waiting for transfers between devices, on_device(): up_share = lax.all_gather(up_weight, 'tm', axis=0, tiled=True)  136 us
    all_gather x1, waiting for transfers between devices, on_device(): down_share = lax.all_gather(down_weight, 'tm', axis=1, tiled=True)  135 us
    another operation x1, loops' own time, carried_in(): return lax.fori_loop(0, count - 1, hop, running)  81.7 us
    dynamic_slice x127, local copies, waits for them, and re-layouts, hop(): longer = join(running, pieces[position])  75.4 us
    unnamed x1, blocking collectives  20.8 us
    unnamed x18, local copies, waits for them, and re-layouts  16.3 us
    all_to_all x1, starting transfers between devices, on_device(): lax.all_to_all(send_rows, 'tm', split_axis=0, concat_axis=0, tiled=True)  15.6 us
    all_to_all x1, starting transfers between devices, on_device(): lax.all_to_all(send_slots, 'tm', split_axis=0, concat_axis=0, tiled=True)  15 us
  transfers between devices with their start and end apart: 8, of which 5 were waited for; matrix products, arithmetic and copies ran while one was open for 19% of the time, Pallas kernels for 0%

commit v1 on v0

v1 whole, which is shorter than its diff:
```python
import jax
import jax.numpy as jnp
import numpy as np
from jax import lax
from jax.sharding import Mesh, PartitionSpec as P

MRG_FRAME = 64
AUD_TOK = 64
SEQ_DEV = 96
D_ENC = 1280
TM = ("z", "y", "c")
NZ, NY, NC, NM = 16, 4, 2, 4
N_TM = NZ * NY * NC
BF = jnp.bfloat16
F32 = jnp.float32


def feature_order():
    block = np.arange(N_TM)
    c, y, z = block // (NY * NZ), (block // NZ) % NY, block % NZ
    first = 10 * (8 * z + 2 * y + c)
    main = (first[:, None] + np.arange(8)[None, :]).reshape(-1)
    rest = (first[None, :] + 8 + np.arange(2)[:, None]).reshape(-1)
    return np.concatenate([main, rest]).astype(np.int32)


def gather(value, axis):
    peers = lax.axis_size(axis)
    spread = jnp.broadcast_to(value[None], (peers,) + value.shape)
    return lax.all_to_all(spread, axis, 0, 0)


def layer_norm(values, scale_gain):
    average = jnp.mean(values, axis=-1, keepdims=True)
    centred = values - average
    variance = jnp.mean(centred * centred, axis=-1, keepdims=True)
    return centred * lax.rsqrt(variance + 1e-05) * scale_gain


def rms_norm(values, scale_gain):
    square_mean = jnp.mean(values * values, axis=-1, keepdims=True)
    return values * lax.rsqrt(square_mean + 1e-06) * scale_gain


def halo(shard):
    up = [(i, i + 1) for i in range(N_TM - 1)]
    down = [(j, i) for i, j in up]
    before = lax.ppermute(shard[-1:], TM, up)
    after = lax.ppermute(shard[:1], TM, down)
    return jnp.concatenate([before, shard, after], axis=0)


def dot(a, b):
    return jnp.dot(a, b, preferred_element_type=F32)


def on_device(
    filterbank,
    conv_weight,
    mlp_gain,
    up_weight,
    down_weight,
    post_gain,
    audio_weight,
    patches,
    vision_gain,
    vision_weight,
    retention,
    kept_count,
):
    down_rows = down_weight.T
    rest = jnp.stack([up_weight[8:], down_rows[8:]])
    rest = rest.reshape(4, 2, 640).transpose(1, 0, 2).reshape(8, 640)
    ffn = jnp.concatenate([up_weight[:8], down_rows[:8], rest], axis=1)
    ffn = gather(ffn, "z")
    count_lane = jnp.broadcast_to(kept_count.astype(BF)[:, None], (40, 64))
    vis = jnp.concatenate([vision_weight, count_lane], axis=1)
    vis = gather(vis, "z")
    ffn = gather(ffn, "y")
    ffn = gather(ffn, "c").reshape(8 * N_TM, 3200)

    order = jnp.asarray(feature_order())
    pick = (lax.broadcasted_iota(jnp.int32, (D_ENC, D_ENC), 0) == order[None, :]).astype(BF)
    conv = dot(conv_weight, pick).astype(BF)
    audio_rows = lax.dot_general(
        pick, audio_weight, (((0,), (0,)), ((), ())), preferred_element_type=F32
    ).astype(BF)
    gains = jnp.dot(
        jnp.stack([mlp_gain, post_gain]), pick.astype(F32), precision=lax.Precision.HIGHEST
    )

    framed = halo(filterbank)
    unfolded = jnp.concatenate([framed[:-2], framed[1:-1], framed[2:]], axis=1)
    stem = jax.nn.gelu(dot(unfolded, conv), approximate=False).astype(BF)
    residual = stem.astype(F32)
    hidden = layer_norm(residual, gains[0]).astype(BF)
    pooled_stem = residual.reshape(64, 2, D_ENC).mean(axis=1)

    rest = ffn[:, 2560:].reshape(N_TM, 2, 4, 640).transpose(2, 0, 1, 3).reshape(4 * N_TM, 1280)
    pre_act = dot(hidden[:, :1024], ffn[:, :1280]) + dot(hidden[:, 1024:], rest[:256])
    activated = jax.nn.gelu(pre_act, approximate=False)
    activated = activated.reshape(64, 2, 1280).mean(axis=1).astype(BF)
    nt = (((1,), (1,)), ((), ()))
    partial_main = lax.dot_general(activated, ffn[:, 1280:2560], nt, preferred_element_type=F32)
    partial_rest = lax.dot_general(activated, rest[256:], nt, preferred_element_type=F32)
    part = jnp.concatenate([partial_main, partial_rest], axis=1)
    sent = part.astype(BF)
    total = part
    for shift in (1, 3, 2):
        moved = lax.ppermute(sent, "mod", [(i, (i + shift) % NM) for i in range(NM)])
        total = total + moved.astype(F32)
    normed = layer_norm(pooled_stem + total, gains[1]).astype(BF)
    audio_tokens = dot(normed, audio_rows).astype(BF)

    vis = gather(vis, "y")
    vis = gather(vis, "c")
    counts = vis[:, :, :, 0, 448].astype(jnp.int32).transpose(2, 1, 0).reshape(N_TM)
    patch_normed = rms_norm(patches.astype(F32), vision_gain).astype(BF)
    merged = patch_normed.reshape(MRG_FRAME, -1)
    vis_rows = vis.transpose(2, 1, 0, 3, 4).reshape(5120, 512)
    visual_tokens = dot(merged, vis_rows)[:, :448].astype(BF)

    me = lax.axis_index(TM).astype(jnp.int32)
    ids = jnp.arange(N_TM, dtype=jnp.int32)
    placed = counts + AUD_TOK
    starts = jnp.sum(jnp.where(ids[None, :] < ids[:, None], placed[None, :], 0), axis=1)
    kept = kept_count[0]
    first_slot = jnp.sum(jnp.where(ids < me, placed, 0))

    local = ((ids - first_slot) % N_TM)[:, None]
    ranks = jnp.arange(MRG_FRAME, dtype=jnp.int32)
    by_rank = (retention[0][:, None] == ranks[None, :]).astype(BF)
    ordered = dot(by_rank, visual_tokens).astype(BF)
    take_visual = ((local == ranks[None, :]) & (ranks[None, :] < kept)).astype(BF)
    take_audio = (local - kept == ranks[None, :]).astype(BF)
    send = dot(
        jnp.concatenate([take_visual, take_audio], axis=1),
        jnp.concatenate([ordered, audio_tokens], axis=0),
    ).astype(BF)
    moved = lax.all_to_all(send.reshape(NZ, NY * NC, 448), "z", 0, 0)
    moved = lax.all_to_all(moved.transpose(1, 0, 2), ("y", "c"), 0, 0)
    moved = moved.reshape(N_TM, 448)

    began = starts.reshape(NZ, NY * NC).T.reshape(N_TM)
    length = placed.reshape(NZ, NY * NC).T.reshape(N_TM)
    offset = (me - began) % N_TM
    slot = jnp.where(offset < length, (began + offset) // N_TM, -1)
    slots = jnp.arange(SEQ_DEV, dtype=jnp.int32)
    put = (slot[None, :] == slots[:, None]).astype(BF)
    return dot(put, moved).astype(BF)[None]


def solution(mesh):
    split = Mesh(mesh.devices.reshape(NZ, NY, NC, NM), TM + ("mod",))
    return jax.shard_map(
        on_device,
        mesh=split,
        in_specs=(
            P(TM, None),
            P(),
            P(),
            P(TM, "mod"),
            P("mod", TM),
            P(),
            P(None, "mod"),
            P(TM, None),
            P(),
            P(TM, "mod"),
            P(TM, None),
            P(TM),
        ),
        out_specs=P(TM, None, "mod"),
        check_vma=False,
    )
```

time: 574 us -> 278 us (0.48); the launches traced: 566 us -> 277 us
  waiting for transfers between devices: 288 us -> 97.9 us
  loops' own time: 81.7 us -> 0 us
  local copies, waits for them, and re-layouts: 97.5 us -> 30.6 us
  blocking collectives: 20.8 us -> 73.5 us
  between operations: 14 us -> 1.34 us
  starting transfers between devices: 40.7 us -> 49.9 us
    all_gather x3 -> x0, waiting for transfers between devices: 271 us -> none  [the longest x1 136 us: on_device(): up_share = lax.all_gather(up_weight, 'tm', axis=0, tiled=True)]
    another operation x1 -> x0, loops' own time: 81.7 us -> none  [carried_in(): return lax.fori_loop(0, count - 1, hop, running)]
    all_to_all x2 -> x5, waiting for transfers between devices: 14.2 us -> 92.5 us  [the longest x3 76 us: gather(): return lax.all_to_all(spread, axis, 0, 0)]
    dynamic_slice x127 -> x0, local copies, waits for them, and re-layouts: 75.4 us -> none  [hop(): longer = join(running, pieces[position])]
    all_to_all x0 -> x3, blocking collectives: none -> 73.5 us  [gather(): return lax.all_to_all(spread, axis, 0, 0)]
    unnamed x1 -> x0, blocking collectives: 20.8 us -> none
    unnamed x18 -> x29, local copies, waits for them, and re-layouts: 16.3 us -> 3.1 us
    broadcast_in_dim x0 -> x6, local copies, waits for them, and re-layouts: none -> 9.83 us  [gather(): spread = jnp.broadcast_to(value[None], (peers,) + value.shape)]
  transfers between devices with their start and end apart: 8 -> 10, of which waited for: 5 -> 7; matrix products, arithmetic and copies ran while one was open for 19% -> 9% of each run, Pallas kernels for 0% -> 0%
where the time goes in v1:
time: 278 us; the launch traced here: 277 us
  waiting for transfers between devices  97.9 us (35%)
  blocking collectives  73.5 us (26%)
  starting transfers between devices  49.9 us (18%)
  local copies, waits for them, and re-layouts  30.6 us (11%)
  matrix products  18.4 us (7%)
  other arithmetic  5.24 us (2%)
    all_to_all x3, waiting for transfers between devices, gather(): return lax.all_to_all(spread, axis, 0, 0)  76 us
    all_to_all x3, blocking collectives, gather(): return lax.all_to_all(spread, axis, 0, 0)  73.5 us
    all_to_all x3, starting transfers between devices, gather(): return lax.all_to_all(spread, axis, 0, 0)  19 us
    dot_general x8, matrix products, dot(): return jnp.dot(a, b, preferred_element_type=F32)  13.3 us
    all_to_all x1, waiting for transfers between devices, on_device(): moved = lax.all_to_all(send.reshape(NZ, NY * NC, 448), 'z', 0, 0)  11.2 us
    ppermute x3, starting transfers between devices, on_device(): lax.ppermute(sent, 'mod', [(i, (i + shift) % NM) for i in range(NM)])  9.93 us
    broadcast_in_dim x6, local copies, waits for them, and re-layouts, gather(): spread = jnp.broadcast_to(value[None], (peers,) + value.shape)  9.83 us
    all_to_all x1, starting transfers between devices, on_device(): moved = lax.all_to_all(send.reshape(NZ, NY * NC, 448), 'z', 0, 0)  7.72 us
  transfers between devices with their start and end apart: 10, of which 7 were waited for; matrix products, arithmetic and copies ran while one was open for 9% of the time, Pallas kernels for 0%

profile of v1, /device:TPU:1, one launch (start us, length us, event | category | flops | bytes accessed | tf_op | source)
XLA Modules:
  0.0 277.0 jit_solution(9953328567876123196)
XLA Ops:
  0.8 0.8 concatenate.28
  1.6 49.6 %all_to_all.40 = bf16[16,40,512]{2,1,0:T(8,128)(2,1)S(1)} all-to-all(bf16[16,40,512]{2,1,0:T(8,128)(2,1)S(1)} %broadcast_in_dim.27), channel_id=1, replica_groups=mesh['z'=16,'y'=4,'c'=2,'mod'=4] {'z'}, dimensions={0} | all-to-all | bytes 1310720 | tf_op jit(solution)/shard_map/all_to_all | solution.py:30
  51.2 1.7 broadcast_in_dim.28
  53.0 4.7 %all-to-all-start.1 = ((bf16[4,16,40,512]{3,2,1,0:T(8,128)(2,1)}), bf16[4,16,40,512]{3,2,1,0:T(8,128)(2,1)}, u32[]{:S(2)}, u32[]{:S(2)}) async-start(bf16[4,16,40,512]{3,2,1,0:T(8,128)(2,1)} %broadcast_in_dim.28), calls=%async_computation.1 | async-start | bytes 5242880 | tf_op jit(solution)/shard_map/all_to_all | solution.py:30
  57.9 28.5 %all-to-all-done.1 = bf16[4,16,40,512]{3,2,1,0:T(8,128)(2,1)} async-done(((bf16[4,16,40,512]{3,2,1,0:T(8,128)(2,1)}), bf16[4,16,40,512]{3,2,1,0:T(8,128)(2,1)}, u32[]{:S(2)}, u32[]{:S(2)}) %all-to-all-start.1) | async-done | bytes 2621472 | tf_op jit(solution)/shard_map/all_to_all | solution.py:30
  86.4 1.0 broadcast_in_dim.32
  87.4 9.5 %all-to-all-start.3 = ((bf16[16,8,3200]{2,1,0:T(8,128)(2,1)}), bf16[16,8,3200]{2,1,0:T(8,128)(2,1)S(1)}, u32[]{:S(2)}, u32[]{:S(2)}) async-start(bf16[16,8,3200]{2,1,0:T(8,128)(2,1)} %broadcast_in_dim.32), calls=%async_computation.3 | async-start | bytes 1638400 | tf_op jit(solution)/shard_map/all_to_all | solution.py:30
  96.9 3.8 %collective-permute-start.1 = (bf16[1,128]{1,0:T(2,128)(2,1)S(1)}, bf16[1,128]{1,0:T(2,128)(2,1)S(1)}, u32[]{:S(2)}, u32[]{:S(2)}) collective-permute-start(bf16[1,128]{1,0:T(2,128)(2,1)S(1)} %get-tuple-element.12), channel_id=1, source_target_pairs={{4,0},{8,4},{12,8},{16,12},{20,16},{24,20},{28,24},{32,28},{36,32}... | collective-permute-start | bytes 776 | tf_op jit(solution)/shard_map/ppermute | solution.py:49
  100.6 2.2 collective-permute-start
  103.7 2.1 fusion.1
  105.9 3.6 %copy.56 = bf16[4,16,40,512]{3,2,0,1:T(8,128)(2,1)} copy(bf16[4,16,40,512]{3,2,1,0:T(8,128)(2,1)} %all-to-all-done.1) | data formatting | bytes 5242880 | tf_op jit(solution)/shard_map/all_to_all | solution.py:30
  109.5 23.1 %all-to-all-done.3 = bf16[16,8,3200]{2,1,0:T(8,128)(2,1)S(1)} async-done(((bf16[16,8,3200]{2,1,0:T(8,128)(2,1)}), bf16[16,8,3200]{2,1,0:T(8,128)(2,1)S(1)}, u32[]{:S(2)}, u32[]{:S(2)}) %all-to-all-start.3) | async-done | bytes 819232 | tf_op jit(solution)/shard_map/all_to_all | solution.py:30
  132.6 2.4 broadcast_in_dim.29
  134.9 14.0 %all_to_all.41 = bf16[2,4,16,40,512]{4,3,1,2,0:T(8,128)(2,1)} all-to-all(bf16[2,4,16,40,512]{4,3,1,2,0:T(8,128)(2,1)S(1)} %broadcast_in_dim.29), channel_id=1, replica_groups=mesh['z'=16,'y'=4,'c'=2,'mod'=4] {'c'}, dimensions={0} | all-to-all | bytes 10485760 | tf_op jit(solution)/shard_map/all_to_all | solution.py:30
  148.9 2.0 broadcast_in_dim.33
  150.9 4.9 %all-to-all-start.4 = ((bf16[4,16,8,3200]{3,2,1,0:T(8,128)(2,1)}), bf16[4,16,8,3200]{3,2,1,0:T(8,128)(2,1)}, u32[]{:S(2)}, u32[]{:S(2)}) async-start(bf16[4,16,8,3200]{3,2,1,0:T(8,128)(2,1)} %broadcast_in_dim.33), calls=%async_computation.4 | async-start | bytes 6553600 | tf_op jit(solution)/shard_map/all_to_all | solution.py:30
  155.8 4.7 %fusion.92 = (f32[128]{0:T(128)S(1)}, f32[128,1280]{1,0:T(8,128)S(1)}) fusion(bf16[384,1280]{1,0:T(8,128)(2,1)} %param.14, s32[1280]{0:T(1024)S(1)} %copy-done.12, bf16[1,128]{1,0:T(2,128)(2,1)S(1)} %collective-permute-done.1, bf16[128,128]{1,0:T(8,128)(2,1)S(1)} %copy-done.11, bf16[1,128]{1,0:T(2,128)(2,1)S(1)} %collective-permute-done), kind=kOutput, calls=%fused_computation.144 | convolution fusion | flops 1399357312 | bytes 1677312 | tf_op jit(solution)/shard_map/dot_general | solution.py:54
  160.8 1.5 reduce_sum.84
  162.8 1.2 slice.87
  164.1 3.2 %copy.61 = bf16[2,4,16,40,512]{4,3,0,1,2:T(8,128)(2,1)S(1)} copy(bf16[2,4,16,40,512]{4,3,1,2,0:T(8,128)(2,1)} %all_to_all.41) | data formatting | bytes 10485760 | tf_op jit(solution)/shard_map/all_to_all | solution.py:30
  167.3 0.7 select_reduce_fusion.1
  168.0 0.6 and_select_fusion
  168.7 1.0 fusion.95
  169.9 24.4 %all-to-all-done.4 = bf16[4,16,8,3200]{3,2,1,0:T(8,128)(2,1)} async-done(((bf16[4,16,8,3200]{3,2,1,0:T(8,128)(2,1)}), bf16[4,16,8,3200]{3,2,1,0:T(8,128)(2,1)}, u32[]{:S(2)}, u32[]{:S(2)}) %all-to-all-start.4) | async-done | bytes 3276832 | tf_op jit(solution)/shard_map/all_to_all | solution.py:30
  194.3 2.8 broadcast_in_dim.34
  197.1 10.0 %all_to_all.42 = bf16[2,4,16,8,3200]{4,3,2,1,0:T(8,128)(2,1)S(1)} all-to-all(bf16[2,4,16,8,3200]{4,3,2,1,0:T(8,128)(2,1)S(1)} %broadcast_in_dim.34), channel_id=1, replica_groups=mesh['z'=16,'y'=4,'c'=2,'mod'=4] {'c'}, dimensions={0} | all-to-all | bytes 13107200 | tf_op jit(solution)/shard_map/all_to_all | solution.py:30
  207.1 2.7 copy-done.1
  209.8 1.2 slice.95
  211.0 2.6 reshape.178
  213.6 0.9 fusion.90
  214.5 0.5 copy.64
  215.1 0.5 copy.63
  216.0 3.6 %fusion.32 = f32[128,1280]{1,0:T(8,128)S(1)} fusion(f32[128,1280]{1,0:T(8,128)S(1)} %fusion.69, bf16[1024,3200]{1,0:T(8,128)(2,1)} %bitcast.46, bf16[128,1280]{1,0:T(8,128)(2,1)} %copy-done.4), kind=kOutput, calls=%fused_computation.33 | convolution fusion | flops 346193920 | bytes 4194304 | tf_op jit(solution)/shard_map/dot_general | solution.py:54
  220.0 0.8 reduce_sum.87
  220.7 2.7 fusion.12
  223.8 4.6 %collective-permute-start.4 = (bf16[64,1280]{1,0:T(8,128)(2,1)S(1)}, bf16[64,1280]{1,0:T(8,128)(2,1)S(1)}, u32[]{:S(2)}, u32[]{:S(2)}) collective-permute-start(bf16[64,1280]{1,0:T(8,128)(2,1)S(1)} %fusion.54), channel_id=1, source_target_pairs={{0,2},{1,3},{2,0},{3,1},{4,6},{5,7},{6,4},{7,5},{8,10},{9,11},{10,... | collective-permute-start | bytes 491528 | tf_op jit(solution)/shard_map/ppermute | solution.py:110
  228.5 2.8 collective-permute-start.3
  231.2 2.5 collective-permute-start.2
  233.9 2.6 collective-permute-done.3
  236.4 2.8 %collective-permute-done.2 = bf16[64,1280]{1,0:T(8,128)(2,1)S(1)} collective-permute-done((bf16[64,1280]{1,0:T(8,128)(2,1)S(1)}, bf16[64,1280]{1,0:T(8,128)(2,1)S(1)}, u32[]{:S(2)}, u32[]{:S(2)}) %collective-permute-start.2) | collective-permute-done | bytes 163872 | tf_op jit(solution)/shard_map/ppermute | solution.py:110
  239.7 2.5 fusion.27
  242.5 0.8 copy.65
  243.2 7.7 %all-to-all-start.6 = ((bf16[16,8,448]{2,1,0:T(8,128)(2,1)}), bf16[16,8,448]{2,1,0:T(8,128)(2,1)S(1)}, u32[]{:S(2)}, u32[]{:S(2)}) async-start(bf16[16,8,448]{2,1,0:T(8,128)(2,1)} %bitcast.17), calls=%async_computation.6 | async-start | bytes 262144 | tf_op jit(solution)/shard_map/all_to_all | solution.py:140
  251.7 11.2 %all-to-all-done.6 = bf16[16,8,448]{2,1,0:T(8,128)(2,1)S(1)} async-done(((bf16[16,8,448]{2,1,0:T(8,128)(2,1)}), bf16[16,8,448]{2,1,0:T(8,128)(2,1)S(1)}, u32[]{:S(2)}, u32[]{:S(2)}) %all-to-all-start.6) | async-done | bytes 114720 | tf_op jit(solution)/shard_map/all_to_all | solution.py:140
  262.9 0.7 copy.66
  263.6 7.3 %all-to-all-start.7 = ((bf16[8,16,448]{2,1,0:T(8,128)(2,1)}), bf16[8,16,448]{2,1,0:T(8,128)(2,1)S(1)}, u32[]{:S(2)}, u32[]{:S(2)}) async-start(bf16[8,16,448]{2,1,0:T(8,128)(2,1)} %copy.66), calls=%async_computation.7 | async-start | bytes 262144 | tf_op jit(solution)/shard_map/all_to_all | solution.py:141
  271.0 5.2 %all-to-all-done.7 = bf16[8,16,448]{2,1,0:T(8,128)(2,1)S(1)} async-done(((bf16[8,16,448]{2,1,0:T(8,128)(2,1)}), bf16[8,16,448]{2,1,0:T(8,128)(2,1)S(1)}, u32[]{:S(2)}, u32[]{:S(2)}) %all-to-all-start.7) | async-done | bytes 114720 | tf_op jit(solution)/shard_map/all_to_all | solution.py:141
  276.2 0.8 fusion.26
  (77 shorter events, 4.9 us)
Async XLA Ops:
  0.0 239.7 %copy-start = (bf16[1280,448]{0,1:T(8,128)(2,1)S(1)}, bf16[1280,448]{0,1:T(8,128)(2,1)}, u32[]{:S(2)}) copy-start(bf16[1280,448]{0,1:T(8,128)(2,1)} %param.19) | copy-start | bytes 3440644
  52.9 4.8 %copy-start.6 = (bf16[1280,10]{0,1:T(8,128)(2,1)S(1)}, bf16[1280,10]{0,1:T(8,128)(2,1)}, u32[]{:S(2)}) copy-start(bf16[1280,10]{0,1:T(8,128)(2,1)} %param.17) | copy-start | bytes 76804
  52.9 4.8 %copy-start.5 = (bf16[10,1280]{1,0:T(8,128)(2,1)S(1)}, bf16[10,1280]{1,0:T(8,128)(2,1)}, u32[]{:S(2)}) copy-start(bf16[10,1280]{1,0:T(8,128)(2,1)} %param.16) | copy-start | bytes 76804
  53.0 4.9 %slice-start = ((bf16[10,1280]{1,0:T(8,128)(2,1)}), bf16[8,1280]{1,0:T(8,128)(2,1)S(1)}, s32[]{:S(2)}) async-start(bf16[10,1280]{1,0:T(8,128)(2,1)} %param.16), calls=%async_computation.8 | async-start | bytes 40960 | tf_op jit(solution)/shard_map/slice | solution.py:74
  53.0 33.4 %all-to-all-start.1 = ((bf16[4,16,40,512]{3,2,1,0:T(8,128)(2,1)}), bf16[4,16,40,512]{3,2,1,0:T(8,128)(2,1)}, u32[]{:S(2)}, u32[]{:S(2)}) async-start(bf16[4,16,40,512]{3,2,1,0:T(8,128)(2,1)} %broadcast_in_dim.28), calls=%async_computation.1 | async-start | bytes 5242880 | tf_op jit(solution)/shard_map/all_to_all | solution.py:30
  57.6 39.2 %copy-start.11 = (bf16[128,128]{1,0:T(8,128)(2,1)S(1)}, bf16[128,128]{1,0:T(8,128)(2,1)}, u32[]{:S(2)}) copy-start(bf16[128,128]{1,0:T(8,128)(2,1)} %param.13) | copy-start | bytes 98308
  57.7 45.1 %copy-start.8 = (f32[1280]{0:T(1024)S(1)}, f32[1280]{0:T(1024)}, u32[]{:S(2)}) copy-start(f32[1280]{0:T(1024)} %param.18) | copy-start | bytes 15364
  57.7 45.1 %copy-start.9 = (f32[1280]{0:T(1024)S(1)}, f32[1280]{0:T(1024)}, u32[]{:S(2)}) copy-start(f32[1280]{0:T(1024)} %param.15) | copy-start | bytes 15364
  57.7 45.2 %copy-start.2 = (bf16[256,1280]{1,0:T(8,128)(2,1)S(1)}, bf16[256,1280]{1,0:T(8,128)(2,1)}, u32[]{:S(2)}) copy-start(bf16[256,1280]{1,0:T(8,128)(2,1)} %param.20) | copy-start | bytes 1966084
  57.7 45.4 %copy-start.7 = (f32[1280]{0:T(1024)S(1)}, f32[1280]{0:T(1024)}, u32[]{:S(2)}) copy-start(f32[1280]{0:T(1024)} %param.21) | copy-start | bytes 15364
  87.3 16.4 %copy-start.12 = (s32[1280]{0:T(1024)S(1)}, s32[1280]{0:T(1024)}, u32[]{:S(2)}) copy-start(s32[1280]{0:T(1024)} %constant.139.clone) | copy-start | bytes 15364
  87.4 45.2 %all-to-all-start.3 = ((bf16[16,8,3200]{2,1,0:T(8,128)(2,1)}), bf16[16,8,3200]{2,1,0:T(8,128)(2,1)S(1)}, u32[]{:S(2)}, u32[]{:S(2)}) async-start(bf16[16,8,3200]{2,1,0:T(8,128)(2,1)} %broadcast_in_dim.32), calls=%async_computation.3 | async-start | bytes 1638400 | tf_op jit(solution)/shard_map/all_to_all | solution.py:30
  96.9 58.9 %collective-permute-start.1 = (bf16[1,128]{1,0:T(2,128)(2,1)S(1)}, bf16[1,128]{1,0:T(2,128)(2,1)S(1)}, u32[]{:S(2)}, u32[]{:S(2)}) collective-permute-start(bf16[1,128]{1,0:T(2,128)(2,1)S(1)} %get-tuple-element.12), channel_id=1, source_target_pairs={{4,0},{8,4},{12,8},{16,12},{20,16},{24,20},{28,24},{32,28},{36,32}... | collective-permute-start | bytes 776 | tf_op jit(solution)/shard_map/ppermute | solution.py:49
  100.6 55.2 %collective-permute-start = (bf16[1,128]{1,0:T(2,128)(2,1)S(1)}, bf16[1,128]{1,0:T(2,128)(2,1)S(1)}, u32[]{:S(2)}, u32[]{:S(2)}) collective-permute-start(bf16[1,128]{1,0:T(2,128)(2,1)S(1)} %get-tuple-element.11), channel_id=1, source_target_pairs={{0,4},{4,8},{8,12},{12,16},{16,20},{20,24},{24,28},{28,32},{32,36}... | collective-permute-start | bytes 776 | tf_op jit(solution)/shard_map/ppermute | solution.py:48
  150.9 43.5 %all-to-all-start.4 = ((bf16[4,16,8,3200]{3,2,1,0:T(8,128)(2,1)}), bf16[4,16,8,3200]{3,2,1,0:T(8,128)(2,1)}, u32[]{:S(2)}, u32[]{:S(2)}) async-start(bf16[4,16,8,3200]{3,2,1,0:T(8,128)(2,1)} %broadcast_in_dim.33), calls=%async_computation.4 | async-start | bytes 6553600 | tf_op jit(solution)/shard_map/all_to_all | solution.py:30
  162.8 52.9 %copy-start.4 = (bf16[128,1280]{1,0:T(8,128)(2,1)}, bf16[128,1280]{1,0:T(8,128)(2,1)S(1)}, u32[]{:S(2)}) copy-start(bf16[128,1280]{1,0:T(8,128)(2,1)S(1)} %multiply_convert_fusion) | copy-start | bytes 983044
  168.7 1.0 copy-start.10
  207.1 2.7 copy-start.1
  220.7 18.5 %copy-start.3 = (f32[64,1280]{1,0:T(8,128)S(1)}, f32[64,1280]{1,0:T(8,128)}, u32[]{:S(2)}) copy-start(f32[64,1280]{1,0:T(8,128)} %reduce_sum.84) | copy-start | bytes 983044
  223.8 10.0 %collective-permute-start.4 = (bf16[64,1280]{1,0:T(8,128)(2,1)S(1)}, bf16[64,1280]{1,0:T(8,128)(2,1)S(1)}, u32[]{:S(2)}, u32[]{:S(2)}) collective-permute-start(bf16[64,1280]{1,0:T(8,128)(2,1)S(1)} %fusion.54), channel_id=1, source_target_pairs={{0,2},{1,3},{2,0},{3,1},{4,6},{5,7},{6,4},{7,5},{8,10},{9,11},{10,... | collective-permute-start | bytes 491528 | tf_op jit(solution)/shard_map/ppermute | solution.py:110
  228.5 8.0 %collective-permute-start.3 = (bf16[64,1280]{1,0:T(8,128)(2,1)S(1)}, bf16[64,1280]{1,0:T(8,128)(2,1)S(1)}, u32[]{:S(2)}, u32[]{:S(2)}) collective-permute-start(bf16[64,1280]{1,0:T(8,128)(2,1)S(1)} %fusion.54), channel_id=1, source_target_pairs={{0,3},{1,0},{2,1},{3,2},{4,7},{5,4},{6,5},{7,6},{8,11},{9,8},{10,9... | collective-permute-start | bytes 491528 | tf_op jit(solution)/shard_map/ppermute | solution.py:110
  231.2 8.0 %collective-permute-start.2 = (bf16[64,1280]{1,0:T(8,128)(2,1)S(1)}, bf16[64,1280]{1,0:T(8,128)(2,1)S(1)}, u32[]{:S(2)}, u32[]{:S(2)}) collective-permute-start(bf16[64,1280]{1,0:T(8,128)(2,1)S(1)} %fusion.54), channel_id=1, source_target_pairs={{0,1},{1,2},{2,3},{3,0},{4,5},{5,6},{6,7},{7,4},{8,9},{9,10},{10,1... | collective-permute-start | bytes 491528 | tf_op jit(solution)/shard_map/ppermute | solution.py:110
  243.2 19.7 %all-to-all-start.6 = ((bf16[16,8,448]{2,1,0:T(8,128)(2,1)}), bf16[16,8,448]{2,1,0:T(8,128)(2,1)S(1)}, u32[]{:S(2)}, u32[]{:S(2)}) async-start(bf16[16,8,448]{2,1,0:T(8,128)(2,1)} %bitcast.17), calls=%async_computation.6 | async-start | bytes 262144 | tf_op jit(solution)/shard_map/all_to_all | solution.py:140
  263.6 12.6 %all-to-all-start.7 = ((bf16[8,16,448]{2,1,0:T(8,128)(2,1)}), bf16[8,16,448]{2,1,0:T(8,128)(2,1)S(1)}, u32[]{:S(2)}, u32[]{:S(2)}) async-start(bf16[8,16,448]{2,1,0:T(8,128)(2,1)} %copy.66), calls=%async_computation.7 | async-start | bytes 262144 | tf_op jit(solution)/shard_map/all_to_all | solution.py:141
